TPU v7x, 32 devices: a whole 2x2x4 slice. The times are simulated.
32 devices in a mesh: img: 2 (over y), cls: 4 (over z), emb: 4 (over x, core).
Axes of the slice: x: 2, y: 2, z: 4, core: 2. Of those that a mesh axis runs over, the one named last changes fastest.
Arguments:
- regions: bfloat16 [2048, 1024], P('img', 'emb'), may hold values from -8 to 8
- table: bfloat16 [21504, 1024], P('cls', 'emb'), may hold values from -1 to 1
- shift: float32 [2048], P('img'), may hold values from -0.5 to 0.1
- scale: float32 [2048], P('img'), may hold values from 2 to 20
- labels: int32 [2048], P('img'), may hold values from -1 to 21503, as said below
- valid: int32 [4, 21504], P('img', 'cls'), may hold values 0 or 1
Outputs:
- loss: float32 [], replicated
- region_grad: bfloat16 [2048, 1024], P('img', 'emb')
- table_grad: bfloat16 [21504, 1024], P('cls', 'emb')
Inputs may be any that keep to these rules, and one draw needn't show every extreme that they name: `labels`: -1 marks background; the first region of every image is foreground.
All inputs are finite; a program needn't handle non-finite values. No bound on the sum of `valid` on one device may be relied on, other than what follows from the above.
Results may differ from a plain program's by a relative error of at most 0.0034.
Values may be sent and summed in bfloat16 or wider, within the bound.
A program may use at most 64 MiB of HBM per device.

v0:
```python
import jax
import jax.numpy as jnp
from jax import lax
from jax.sharding import PartitionSpec as P

CLASSES = 21504
REG_IMG = 512


def focal(logit, target):
    prob = jax.nn.sigmoid(logit)
    return -0.25 * target * (1.0 - prob) ** 2 * jax.nn.log_sigmoid(logit) - 0.75 * (
        1.0 - target
    ) * prob**2 * jax.nn.log_sigmoid(-logit)


def shards(regions, table, shift, scale, labels, valid):
    rows = regions.shape[0]
    class_dev = table.shape[0]
    parts = lax.axis_size("emb")
    quarter = rows // parts
    start = lax.axis_index("emb") * quarter
    block = regions.astype(jnp.float32)
    squares = lax.psum(jnp.sum(block * block, axis=1), "emb")
    local_count = jnp.sum((labels >= 0).astype(jnp.float32))
    count = lax.psum(local_count, "img")
    inv = lax.rsqrt(squares + 1e-06)
    unit = block * inv[:, None]
    unit_b = unit.astype(jnp.bfloat16)
    unit_rows = lax.all_to_all(unit_b, "emb", split_axis=0, concat_axis=1, tiled=True)
    cosine = lax.dot_general(
        unit_rows,
        lax.all_gather(table, "emb", axis=1, tiled=True),
        (((1,), (1,)), ((), ())),
        preferred_element_type=jnp.float32,
    )
    shift_q = lax.dynamic_slice_in_dim(shift, start, quarter, 0)
    scale_q = lax.dynamic_slice_in_dim(scale, start, quarter, 0)
    label_q = lax.dynamic_slice_in_dim(labels, start, quarter, 0)
    image_ids = (start + jnp.arange(quarter, dtype=jnp.int32)) // REG_IMG
    onehot = (image_ids[:, None] == jnp.arange(valid.shape[0], dtype=jnp.int32)[None, :]).astype(
        jnp.float32
    )
    mask = jnp.dot(onehot, valid.astype(jnp.float32), preferred_element_type=jnp.float32)
    class_ids = lax.axis_index("cls") * class_dev + jnp.arange(class_dev, dtype=jnp.int32)
    logit = (cosine + shift_q[:, None]) * scale_q[:, None]
    target = (label_q[:, None] == class_ids[None, :]).astype(jnp.float32)
    term, pullback = jax.vjp(lambda value: focal(value, target), logit)
    dlogit = pullback(jnp.ones_like(term))[0]
    total = lax.psum(jnp.sum(term * mask), ("img", "cls", "emb"))
    factor = rows * lax.axis_size("img") / count
    dscore = (dlogit * mask * scale_q[:, None] * factor).astype(jnp.bfloat16)
    piece = lax.all_gather(dscore, "emb", axis=0, tiled=True)
    dunit_piece = jnp.dot(piece, table, preferred_element_type=jnp.float32)
    table_acc = lax.dot_general(
        piece, unit_b, (((0,), (0,)), ((), ())), preferred_element_type=jnp.float32
    )
    dunit = lax.psum(dunit_piece, "cls")
    radial = lax.psum(jnp.sum(unit * dunit, axis=1), "emb")
    region_grad = (inv[:, None] * (dunit - unit * radial[:, None])).astype(jnp.bfloat16)
    table_grad = lax.psum(table_acc, "img").astype(jnp.bfloat16)
    loss = total / count / CLASSES
    return (loss, region_grad, table_grad)


def solution(mesh):
    placed = (P("img", "emb"), P("cls", "emb"), P("img"), P("img"), P("img"), P("img", "cls"))
    return jax.shard_map(
        shards,
        mesh=mesh,
        in_specs=placed,
        out_specs=(P(), P("img", "emb"), P("cls", "emb")),
        check_vma=False,
    )
```

profile of v0, /device:TPU:0, one launch (start us, length us, event | category | flops | bytes accessed | tf_op | source)
XLA Modules:
  0.0 357.9 jit_solution(13751728279272978331)
XLA Ops:
  7.2 0.7 all-gather.3.cloned.1.call-update
  7.9 1.3 fusion.33
  9.2 8.4 %psum.42 = f32[1024]{0:T(1024)S(1)} all-reduce(f32[1024]{0:T(1024)S(1)} %fusion.33), channel_id=1, replica_groups=mesh['img'=2,'cls'=4,'emb'=4] {'emb'}, use_global_device_ids=true, to_apply=%region_1.0 | all-reduce | flops 1024 | bytes 8192 | tf_op jit(solution)/shard_map/psum | solution.py:24
  17.6 1.3 fusion.28
  18.9 1.0 copy.9
  19.9 3.5 all-to-all-start
  23.4 0.0 all-gather.5.cloned.1.call-start
  23.5 0.6 convert_reduce_fusion
  24.1 5.5 %psum.44 = f32[]{:T(128)} all-reduce(f32[]{:T(128)} %convert_reduce_fusion), channel_id=1, replica_groups=mesh['img'=2,'cls'=4,'emb'=4] {'img'}, use_global_device_ids=true, to_apply=%region_5.7 | all-reduce | flops 1 | bytes 8 | tf_op jit(solution)/shard_map/psum | solution.py:26
  29.6 0.1 dynamic_slice.9
  29.7 0.8 dynamic_slice.11
  30.5 0.8 dynamic_slice.10
  31.9 6.3 %all-to-all-done = bf16[4,256,256]{1,2,0:T(8,128)(2,1)S(1)} async-done(((bf16[4,256,256]{1,2,0:T(8,128)(2,1)}), bf16[4,256,256]{1,2,0:T(8,128)(2,1)S(1)}, u32[]{:S(2)}, u32[]{:S(2)}) %all-to-all-start) | async-done | bytes 524320 | tf_op jit(solution)/shard_map/all_to_all | solution.py:30
  38.2 54.3 %all-gather.3.cloned.1.call-done = bf16[5376,1024]{1,0:T(8,128)(2,1)} async-done(((bf16[5376,256]{1,0:T(8,128)(2,1)}), bf16[5376,1024]{1,0:T(8,128)(2,1)}) %all-gather.3.cloned.1.call-update) | async-done | bytes 11010064 | tf_op jit(solution)/shard_map/all_gather | solution.py:33
  92.5 6.5 %fusion = f32[256,5376]{1,0:T(8,128)S(1)} fusion(bf16[256,1024]{0,1:T(8,128)(2,1)S(1)} %bitcast.11, bf16[5376,1024]{1,0:T(8,128)(2,1)} %all-gather.3.cloned.1.call-done, f32[256]{0:T(256)S(1)} %dynamic_slice.11, f32[256]{0:T(256)S(1)} %dynamic_slice.10), kind=kOutput, calls=%fused_computation.7 | convolution fusion | flops 2821324800 | bytes 17041408 | tf_op jit(solution)/shard_map/dot_general | solution.py:31
  99.1 18.2 %fusion.12 = (bf16[256,5376]{1,0:T(8,128)(2,1)}, f32[]{:T(128)}) fusion(f32[256,5376]{1,0:T(8,128)S(1)} %fusion, f32[]{:T(128)S(6)} %div.31, f32[256]{0:T(256)S(1)} %dynamic_slice.11, s32[5376]{0:T(1024)S(1)} %iota_add_fusion, s32[256]{0:T(256)S(1)} %dynamic_slice.9, s32[2,5376]{1,0:T(2,128)S(1)} %copy-done.3, s32[256]{0:T(256)S(1)} %and_select_fusion), kind=kOutput, calls=%fused_computation.25 | convolution fusion | flops 94972928 | bytes 8325128 | tf_op jit(solution)/shard_map/dot_general | solution.py:44
  117.4 40.5 %psum.43 = f32[]{:T(128)} all-reduce(f32[]{:T(128)} %get-tuple-element.12), channel_id=1, replica_groups=mesh['img'=2,'cls'=4,'emb'=4] {'img','cls','emb'}, use_global_device_ids=true, to_apply=%region_3.5 | all-reduce | flops 1 | bytes 8 | tf_op jit(solution)/shard_map/psum | solution.py:50
  159.2 32.3 %all-gather.5.cloned.1.call-done = bf16[1024,5376]{1,0:T(8,128)(2,1)} async-done(((bf16[256,5376]{1,0:T(8,128)(2,1)}), bf16[1024,5376]{1,0:T(8,128)(2,1)}) %all-gather.5.cloned.1.call-update) | async-done | bytes 11010064 | tf_op jit(solution)/shard_map/all_gather | solution.py:53
  191.5 8.1 %fusion.37 = f32[1024,256]{1,0:T(8,128)} fusion(bf16[1024,5376]{1,0:T(8,128)(2,1)} %all-gather.5.cloned.1.call-done, bf16[5376,256]{1,0:T(8,128)(2,1)S(1)} %copy-done.1), kind=kOutput, calls=%fused_computation.63 | convolution fusion | flops 2818572288 | bytes 14811136 | tf_op jit(solution)/shard_map/dot_general | solution.py:54
  199.7 9.6 %fusion.38 = f32[5376,256]{1,0:T(8,128)} fusion(bf16[1024,5376]{1,0:T(8,128)(2,1)} %all-gather.5.cloned.1.call-done, bf16[1024,256]{1,0:T(8,128)(2,1)S(1)} %fusion.28), kind=kOutput, calls=%fused_computation.64 | convolution fusion | flops 2818572288 | bytes 17039360 | tf_op jit(solution)/shard_map/dot_general | solution.py:55
  209.2 131.1 %all-reduce.4 = bf16[5376,256]{1,0:T(8,128)(2,1)} all-reduce(f32[5376,256]{1,0:T(8,128)} %fusion.38), channel_id=1, replica_groups=mesh['img'=2,'cls'=4,'emb'=4] {'img'}, use_global_device_ids=true, to_apply=%region_9.11 | all-reduce | flops 1376256 | bytes 8257536 | tf_op jit(solution)/shard_map/psum | solution.py:61
  340.4 1.6 fusion.29
  342.0 5.9 %psum.46 = f32[1024]{0:T(1024)S(1)} all-reduce(f32[1024]{0:T(1024)S(1)} %fusion.29), channel_id=1, replica_groups=mesh['img'=2,'cls'=4,'emb'=4] {'emb'}, use_global_device_ids=true, to_apply=%region_8.10 | all-reduce | flops 1024 | bytes 8192 | tf_op jit(solution)/shard_map/psum | solution.py:59
  347.9 2.4 fusion.32
  (16 shorter events, 0.2 us)
Async XLA Ops:
  7.2 16.3 %copy-start.2 = (s32[1024]{0:T(1024)S(1)}, s32[1024]{0:T(1024)}, u32[]{:S(2)}) copy-start(s32[1024]{0:T(1024)} %param.11) | copy-start | bytes 12292
  7.2 85.4 %all-gather.3.cloned.1.call-start = ((), (), s32[]{:S(2)}) async-start(), calls=%async_computation.1 | async-start | bytes 13762560 | tf_op jit(solution)/shard_map/all_gather | solution.py:33
  19.9 18.4 %all-to-all-start = ((bf16[4,256,256]{1,2,0:T(8,128)(2,1)}), bf16[4,256,256]{1,2,0:T(8,128)(2,1)S(1)}, u32[]{:S(2)}, u32[]{:S(2)}) async-start(bf16[4,256,256]{1,2,0:T(8,128)(2,1)} %copy.9), calls=%async_computation | async-start | bytes 1048576 | tf_op jit(solution)/shard_map/all_to_all | solution.py:30
  23.4 168.1 %all-gather.5.cloned.1.call-start = ((), (), s32[]{:S(2)}) async-start(), calls=%async_computation.2 | async-start | bytes 13762560 | tf_op jit(solution)/shard_map/all_gather | solution.py:53
  92.5 6.5 %copy-start.3 = (s32[2,5376]{1,0:T(2,128)S(1)}, s32[2,5376]{1,0:T(2,128)}, u32[]{:S(2)}) copy-start(s32[2,5376]{1,0:T(2,128)} %param.12) | copy-start | bytes 129028
  99.1 92.4 %copy-start.1 = (bf16[5376,256]{1,0:T(8,128)(2,1)S(1)}, bf16[5376,256]{1,0:T(8,128)(2,1)}, u32[]{:S(2)}) copy-start(bf16[5376,256]{1,0:T(8,128)(2,1)} %param.8) | copy-start | bytes 8257540
  117.3 223.1 %all-reduce.3.cloned.1.call-start = ((), (), s32[]{:S(2)}) async-start(), calls=%async_computation.3 | async-start | bytes 2097152 | tf_op jit(solution)/shard_map/psum | solution.py:58
  209.2 131.2 %copy-start = (bf16[1024,256]{1,0:T(8,128)(2,1)S(1)}, bf16[1024,256]{1,0:T(8,128)(2,1)}, u32[]{:S(2)}) copy-start(bf16[1024,256]{1,0:T(8,128)(2,1)} %param.7) | copy-start | bytes 1572868
Sparse Core Ops, SparseCore 0:
  9.5 82.9 all-gather.2
  117.4 74.0 all-gather.4
  199.8 51.7 all-reduce.2
where the time goes:
time: 359 us; the launch traced here: 358 us
  blocking collectives  191 us (53%)
  waiting for transfers between devices  93.6 us (26%)
  matrix products  42.4 us (12%)
  between operations  17 us (5%)
  other arithmetic  7.16 us (2%)
  starting transfers between devices  3.66 us (1%)
    psum x1, blocking collectives, shards(): table_grad = lax.psum(table_acc, 'img').astype(jnp.bfloat16)  131 us
    all_gather x1, waiting for transfers between devices, shards(): lax.all_gather(table, 'emb', axis=1, tiled=True)  54.3 us
    psum x1, blocking collectives, shards(): total = lax.psum(jnp.sum(term * mask), ('img', 'cls', 'emb'))  40.5 us
    all_gather x1, waiting for transfers between devices, shards(): piece = lax.all_gather(dscore, 'emb', axis=0, tiled=True)  32.3 us
    dot_general x1, matrix products, shards(): jnp.dot(onehot, valid.astype(jnp.float32), preferred_element_type=jnp.flo...  18.2 us
    dot_general x1, matrix products, shards(): lax.dot_general(piece, unit_b, (((0,), (0,)), ((), ())), preferred_elemen...  9.56 us
    psum x1, blocking collectives, shards(): squares = lax.psum(jnp.sum(block * block, axis=1), 'emb')  8.38 us
    dot_general x1, matrix products, shards(): dunit_piece = jnp.dot(piece, table, preferred_element_type=jnp.float32)  8.13 us
  transfers between devices with their start and end apart: 4, of which 3 were waited for; matrix products, arithmetic and copies ran while one was open for 4% of the time, Pallas kernels for 0%

commit v1 on v0

--- a/solution.py
+++ b/solution.py
@@ -30,7 +30,9 @@
     unit_rows = lax.all_to_all(unit_b, "emb", split_axis=0, concat_axis=1, tiled=True)
     cosine = lax.dot_general(
         unit_rows,
-        lax.all_gather(table, "emb", axis=1, tiled=True),
+        jnp.concatenate(
+            lax.all_to_all(jnp.stack([table] * lax.axis_size("emb")), "emb", 0, 0), axis=1
+        ),
         (((1,), (1,)), ((), ())),
         preferred_element_type=jnp.float32,
     )

time: 359 us -> 430 us (1.20)
  waiting for transfers between devices: 93.6 us -> 145 us
  blocking collectives: 191 us -> 203 us
  local copies, waits for them, and re-layouts: 2.61 us -> 8.13 us
    all_to_all x1, waiting for transfers between devices: 6.29 us -> 113 us  [shards(): lax.all_to_all(jnp.stack([table] * lax.axis_size('emb')), 'emb', 0, 0)]
    all_gather x1 -> x0, waiting for transfers between devices: 54.3 us -> none  [shards(): lax.all_gather(table, 'emb', axis=1, tiled=True)]
    all_to_all x0 -> x1, blocking collectives: none -> 11.2 us  [shards(): lax.all_to_all(unit_b, 'emb', split_axis=0, concat_axis=1, tiled=True)]
    another operation x0 -> x1, local copies, waits for them, and re-layouts: none -> 6.52 us  [shards(): jnp.stack([table] * lax.axis_size('emb'))]
  transfers between devices with their start and end apart: 4 -> 3, of which waited for: 3 -> 2; matrix products, arithmetic and copies ran while one was open for 4% -> 3% of each run, Pallas kernels for 0% -> 0%
where the time goes in v1:
time: 430 us; the launch traced here: 429 us
  blocking collectives  203 us (47%)
  waiting for transfers between devices  145 us (34%)
  matrix products  41.9 us (10%)
  between operations  17.3 us (4%)
  local copies, waits for them, and re-layouts  8.13 us (2%)
  other arithmetic  7.09 us (2%)
  starting transfers between devices  6.3 us (1%)
    psum x1, blocking collectives, shards(): table_grad = lax.psum(table_acc, 'img').astype(jnp.bfloat16)  131 us
    all_to_all x1, waiting for transfers between devices, shards(): lax.all_to_all(jnp.stack([table] * lax.axis_size('emb')), 'emb', 0, 0)  113 us
    psum x1, blocking collectives, shards(): total = lax.psum(jnp.sum(term * mask), ('img', 'cls', 'emb'))  40.7 us
    all_gather x1, waiting for transfers between devices, shards(): piece = lax.all_gather(dscore, 'emb', axis=0, tiled=True)  32.4 us
    dot_general x1, matrix products, shards(): jnp.dot(onehot, valid.astype(jnp.float32), preferred_element_type=jnp.flo...  18.2 us
    all_to_all x1, blocking collectives, shards(): lax.all_to_all(unit_b, 'emb', split_axis=0, concat_axis=1, tiled=True)  11.2 us
    dot_general x1, matrix products, shards(): lax.dot_general(piece, unit_b, (((0,), (0,)), ((), ())), preferred_elemen...  9.56 us
  transfers between devices with their start and end apart: 3, of which 2 were waited for; matrix products, arithmetic and copies ran while one was open for 3% of the time, Pallas kernels for 0%

profile of v1, /device:TPU:0, one launch (start us, length us, event | category | flops | bytes accessed | tf_op | source)
XLA Modules:
  0.0 428.7 jit_solution(11291862278960100149)
XLA Ops:
  7.2 1.3 fusion.43
  8.4 8.4 %psum.42 = f32[1024]{0:T(1024)S(1)} all-reduce(f32[1024]{0:T(1024)S(1)} %fusion.43), channel_id=1, replica_groups=mesh['img'=2,'cls'=4,'emb'=4] {'emb'}, use_global_device_ids=true, to_apply=%region_1.0 | all-reduce | flops 1024 | bytes 8192 | tf_op jit(solution)/shard_map/psum | solution.py:24
  16.8 1.2 fusion.38
  18.1 11.2 %all_to_all.21 = bf16[4,256,256]{2,1,0:T(8,128)(2,1)S(1)} all-to-all(bf16[4,256,256]{2,1,0:T(8,128)(2,1)S(1)} %bitcast.23), channel_id=1, replica_groups=mesh['img'=2,'cls'=4,'emb'=4] {'emb'}, dimensions={0} | all-to-all | bytes 1048576 | tf_op jit(solution)/shard_map/all_to_all | solution.py:30
  29.3 6.5 %stack.2 = bf16[4,5376,256]{2,1,0:T(8,128)(2,1)} broadcast(bf16[5376,256]{1,0:T(8,128)(2,1)} %param.8), dimensions={1,2} | broadcast | bytes 13762560 | tf_op jit(solution)/shard_map/stack | solution.py:34
  35.8 6.2 %all-to-all-start.1 = ((bf16[4,5376,256]{2,1,0:T(8,128)(2,1)}), bf16[4,5376,256]{2,1,0:T(8,128)(2,1)}, u32[]{:S(2)}, u32[]{:S(2)}) async-start(bf16[4,5376,256]{2,1,0:T(8,128)(2,1)} %stack.2), calls=%async_computation.1 | async-start | bytes 22020096 | tf_op jit(solution)/shard_map/all_to_all | solution.py:34
  42.0 0.0 all-gather.2.cloned.1.call-start
  42.1 0.6 convert_reduce_fusion
  42.7 5.5 %psum.44 = f32[]{:T(128)} all-reduce(f32[]{:T(128)} %convert_reduce_fusion), channel_id=1, replica_groups=mesh['img'=2,'cls'=4,'emb'=4] {'img'}, use_global_device_ids=true, to_apply=%region_5.7 | all-reduce | flops 1 | bytes 8 | tf_op jit(solution)/shard_map/psum | solution.py:26
  48.2 0.1 dynamic_slice.9
  48.3 0.8 dynamic_slice.11
  49.1 0.8 dynamic_slice.10
  50.6 112.7 %all-to-all-done.1 = bf16[4,5376,256]{2,1,0:T(8,128)(2,1)} async-done(((bf16[4,5376,256]{2,1,0:T(8,128)(2,1)}), bf16[4,5376,256]{2,1,0:T(8,128)(2,1)}, u32[]{:S(2)}, u32[]{:S(2)}) %all-to-all-start.1) | async-done | bytes 11010080 | tf_op jit(solution)/shard_map/all_to_all | solution.py:34
  163.3 6.0 %fusion.8 = f32[256,5376]{1,0:T(8,128)S(1)} fusion(bf16[4,5376,256]{2,1,0:T(8,128)(2,1)} %all-to-all-done.1, f32[256]{0:T(256)S(1)} %dynamic_slice.11, f32[256]{0:T(256)S(1)} %dynamic_slice.10, bf16[4,256,256]{2,1,0:T(8,128)(2,1)S(1)} %all_to_all.21), kind=kOutput, calls=%fused_computation.10 | convolution fusion | flops 2821324800 | bytes 17041408 | tf_op jit(solution)/shard_map/dot_general | solution.py:31
  169.3 18.2 %fusion.22 = (bf16[256,5376]{1,0:T(8,128)(2,1)}, f32[]{:T(128)}) fusion(f32[256,5376]{1,0:T(8,128)S(1)} %fusion.8, f32[]{:T(128)S(6)} %div.31, f32[256]{0:T(256)S(1)} %dynamic_slice.11, s32[5376]{0:T(1024)S(1)} %iota_add_fusion, s32[256]{0:T(256)S(1)} %dynamic_slice.9, s32[2,5376]{1,0:T(2,128)S(1)} %copy-done.3, s32[256]{0:T(256)S(1)} %and_select_fusion), kind=kOutput, calls=%fused_computation.28 | convolution fusion | flops 94972928 | bytes 8325128 | tf_op jit(solution)/shard_map/dot_general | solution.py:46
  187.5 0.0 all-reduce.3.cloned.1.call-start
  187.5 40.7 %psum.43 = f32[]{:T(128)} all-reduce(f32[]{:T(128)} %get-tuple-element.12), channel_id=1, replica_groups=mesh['img'=2,'cls'=4,'emb'=4] {'img','cls','emb'}, use_global_device_ids=true, to_apply=%region_3.5 | all-reduce | flops 1 | bytes 8 | tf_op jit(solution)/shard_map/psum | solution.py:52
  229.6 32.4 %all-gather.2.cloned.1.call-done = bf16[1024,5376]{1,0:T(8,128)(2,1)} async-done(((bf16[256,5376]{1,0:T(8,128)(2,1)}), bf16[1024,5376]{1,0:T(8,128)(2,1)}) %all-gather.2.cloned.1.call-update) | async-done | bytes 11010064 | tf_op jit(solution)/shard_map/all_gather | solution.py:55
  262.0 8.1 %fusion.48 = f32[1024,256]{1,0:T(8,128)} fusion(bf16[1024,5376]{1,0:T(8,128)(2,1)} %all-gather.2.cloned.1.call-done, bf16[5376,256]{1,0:T(8,128)(2,1)S(1)} %copy-done.1), kind=kOutput, calls=%fused_computation.67 | convolution fusion | flops 2818572288 | bytes 14811136 | tf_op jit(solution)/shard_map/dot_general | solution.py:56
  270.2 9.6 %fusion.49 = f32[5376,256]{1,0:T(8,128)} fusion(bf16[1024,5376]{1,0:T(8,128)(2,1)} %all-gather.2.cloned.1.call-done, bf16[1024,256]{1,0:T(8,128)(2,1)S(1)} %fusion.38), kind=kOutput, calls=%fused_computation.68 | convolution fusion | flops 2818572288 | bytes 17039360 | tf_op jit(solution)/shard_map/dot_general | solution.py:57
  279.7 131.2 %all-reduce.4 = bf16[5376,256]{1,0:T(8,128)(2,1)} all-reduce(f32[5376,256]{1,0:T(8,128)} %fusion.49), channel_id=1, replica_groups=mesh['img'=2,'cls'=4,'emb'=4] {'img'}, use_global_device_ids=true, to_apply=%region_9.11 | all-reduce | flops 1376256 | bytes 8257536 | tf_op jit(solution)/shard_map/psum | solution.py:63
  410.9 1.6 fusion.39
  412.5 5.9 %psum.46 = f32[1024]{0:T(1024)S(1)} all-reduce(f32[1024]{0:T(1024)S(1)} %fusion.39), channel_id=1, replica_groups=mesh['img'=2,'cls'=4,'emb'=4] {'emb'}, use_global_device_ids=true, to_apply=%region_8.10 | all-reduce | flops 1024 | bytes 8192 | tf_op jit(solution)/shard_map/psum | solution.py:61
  418.4 2.4 fusion.42
  (14 shorter events, 0.1 us)
Async XLA Ops:
  35.8 6.3 %copy-start.2 = (s32[1024]{0:T(1024)S(1)}, s32[1024]{0:T(1024)}, u32[]{:S(2)}) copy-start(s32[1024]{0:T(1024)} %param.11) | copy-start | bytes 12292
  35.8 127.5 %all-to-all-start.1 = ((bf16[4,5376,256]{2,1,0:T(8,128)(2,1)}), bf16[4,5376,256]{2,1,0:T(8,128)(2,1)}, u32[]{:S(2)}, u32[]{:S(2)}) async-start(bf16[4,5376,256]{2,1,0:T(8,128)(2,1)} %stack.2), calls=%async_computation.1 | async-start | bytes 22020096 | tf_op jit(solution)/shard_map/all_to_all | solution.py:34
  42.0 220.0 %all-gather.2.cloned.1.call-start = ((), (), s32[]{:S(2)}) async-start(), calls=%async_computation.2 | async-start | bytes 13762560 | tf_op jit(solution)/shard_map/all_gather | solution.py:55
  50.5 118.7 %copy-start.3 = (s32[2,5376]{1,0:T(2,128)S(1)}, s32[2,5376]{1,0:T(2,128)}, u32[]{:S(2)}) copy-start(s32[2,5376]{1,0:T(2,128)} %param.12) | copy-start | bytes 129028
  169.3 92.7 %copy-start.1 = (bf16[5376,256]{1,0:T(8,128)(2,1)S(1)}, bf16[5376,256]{1,0:T(8,128)(2,1)}, u32[]{:S(2)}) copy-start(bf16[5376,256]{1,0:T(8,128)(2,1)} %param.8) | copy-start | bytes 8257540
  187.5 223.4 %all-reduce.3.cloned.1.call-start = ((), (), s32[]{:S(2)}) async-start(), calls=%async_computation.3 | async-start | bytes 2097152 | tf_op jit(solution)/shard_map/psum | solution.py:60
  279.7 131.2 %copy-start = (bf16[1024,256]{1,0:T(8,128)(2,1)S(1)}, bf16[1024,256]{1,0:T(8,128)(2,1)}, u32[]{:S(2)}) copy-start(bf16[1024,256]{1,0:T(8,128)(2,1)} %param.7) | copy-start | bytes 1572868
Sparse Core Ops, SparseCore 0:
  187.6 74.3 all-gather.1
  270.3 51.7 all-reduce.2
